TPU v7x, 1024 devices: a whole 8x8x8 slice. The times are simulated.
1024 devices in a mesh: kgrp: 64 (over x, z), scr: 16 (over y, core).
Axes of the slice: x: 8, y: 8, z: 8, core: 2. Of those that a mesh axis runs over, the one named last changes fastest.
Arguments:
- wave_val: bfloat16 [64, 32, 2048], P('kgrp', None, 'scr'), may hold values from -6 to 6
- wave_con: bfloat16 [64, 32, 2048], P('kgrp', None, 'scr'), may hold values from -6 to 6
- excite: bfloat16 [64, 1024, 16], P('kgrp', 'scr'), may hold values from -6 to 6
- screening: bfloat16 [64, 2048, 2048], P('kgrp', None, 'scr'), may hold values from -9.1552734e-05 to 9.1552734e-05
- pair_count: int32 [64], P('kgrp'), may hold values from 1 to 2, as said below
- pair_kpoint: int32 [64, 2], P('kgrp'), may hold values from 0 to 63
- pair_partner: int32 [64, 2], P('kgrp'), may hold values from 0 to 63
Outputs:
- forward: float32 [64, 2, 1024, 16], P('kgrp', None, 'scr')
- transposed: float32 [64, 2, 1024, 16], P('kgrp', None, 'scr')
Inputs may be any that keep to these rules, and one draw needn't show every extreme that they name: Slot p of screening owner h is live when p < pair_count[h]; in every draw some owner has 2 live slots.
All inputs are finite; a program needn't handle non-finite values.
Results may differ from a plain program's by a relative error of at most 0.0057.
Values may be sent and summed in bfloat16 or wider, within the bound.
A program may use at most 64 MiB of HBM per device.

v0:
```python
import math

import jax
import jax.numpy as jnp
from jax import lax
from jax.sharding import PartitionSpec as P

PTS_BLK = 128


def in_one_piece(arrays, axis, dim, along):
    widths = [math.prod(a.shape[along:]) for a in arrays]
    both = jnp.concatenate(
        [a.reshape(*a.shape[:along], w) for a, w in zip(arrays, widths)], axis=along
    )
    out = lax.all_gather(both, axis, axis=dim, tiled=True)
    tiles = jnp.split(out, [sum(widths[:k]) for k in range(1, len(widths))], axis=along)
    return tuple((b.reshape(*out.shape[:along], *a.shape[along:]) for a, b in zip(arrays, tiles)))


def laid_out(tiles, dim):
    tiles = jnp.moveaxis(tiles, 0, dim)
    shape = tiles.shape
    return tiles.reshape(*shape[:dim], shape[dim] * shape[dim + 1], *shape[dim + 2 :])


def gather_together(arrays, axis, dims):
    vector = jnp.concatenate([a.reshape(-1) for a in arrays])
    lines, at, done = (lax.all_gather(vector, axis), 0, [])
    for a, dim in zip(arrays, dims):
        tiles = lines[:, at : at + a.size].reshape(-1, *a.shape)
        done.append(laid_out(tiles, dim))
        at += a.size
    return tuple(done)


def split_up(value, dim, count):
    shape = value.shape
    tiles = value.reshape(*shape[:dim], count, shape[dim] // count, *shape[dim + 1 :])
    return jnp.moveaxis(tiles, dim, 0)


def sent_and_summed(value, axis, dim):
    tiles = split_up(value, dim, lax.axis_size(axis))
    arrived = lax.all_to_all(tiles, axis, split_axis=0, concat_axis=0, tiled=True)
    return arrived.sum(axis=0)


def in_one_piece_2(arrays, axis, dim, along):
    both = jnp.concatenate(arrays, axis=along)
    out, at, done = (sent_and_summed(both, axis, dim), 0, [])
    for a in arrays:
        done.append(lax.slice_in_dim(out, at, at + a.shape[along], axis=along))
        at += a.shape[along]
    return tuple(done)


def body(wave_val, wave_con, excite, screening, pair_count, pair_kpoint, pair_partner):
    slots = pair_kpoint.shape[1]
    role_total = 2 * slots
    roles = jnp.concatenate([pair_kpoint[0], pair_partner[0]])
    nval = wave_val.shape[1]
    ncon = wave_con.shape[1]
    mu_dev = wave_val.shape[2]
    rows_dev = excite.shape[1]
    nexc = excite.shape[2]
    pieces = in_one_piece((wave_val, wave_con, excite), "kgrp", 0, 1)
    pieces_here = pieces[0].shape[0]
    kpoint_ids = jnp.arange(pieces_here, dtype=jnp.int32)
    picker = (roles[:, None] == kpoint_ids[None, :]).astype(jnp.bfloat16)
    picked = tuple(
        (
            jnp.dot(picker, piece.reshape(pieces_here, -1), preferred_element_type=jnp.float32)
            for piece in pieces
        )
    )
    sel_val = picked[0].astype(jnp.bfloat16).reshape(role_total, nval, mu_dev)
    sel_con = picked[1].astype(jnp.bfloat16).reshape(role_total, ncon, mu_dev)
    sel_exc = picked[2].astype(jnp.bfloat16).reshape(role_total, rows_dev, nexc)
    full_con, full_exc = gather_together((sel_con, sel_exc), "scr", (2, 1))
    weights = screening[0]
    width_all = full_con.shape[2]
    mu_step = min(width_all, 512)
    mu_blocks = width_all // mu_step
    ahead_list = []
    back_list = []
    for slot_index in range(slots):
        con_first = full_con[slot_index]
        con_second = full_con[slots + slot_index]
        screen_sum = jnp.zeros((ncon * ncon, mu_dev), jnp.float32)
        for part_index in range(mu_blocks):
            lower = part_index * mu_step
            upper = lower + mu_step
            left = con_first[:, lower:upper].astype(jnp.float32)
            right = con_second[:, lower:upper].astype(jnp.float32)
            density = (
                (left[:, None, :] * right[None, :, :])
                .astype(jnp.bfloat16)
                .reshape(ncon * ncon, mu_step)
            )
            screen_sum = screen_sum + jnp.dot(
                density, weights[lower:upper], preferred_element_type=jnp.float32
            )
        screened = screen_sum.astype(jnp.bfloat16)
        val_first = sel_val[slot_index].astype(jnp.float32)
        val_second = sel_val[slots + slot_index].astype(jnp.float32)
        rho_val = (
            (val_first.T[:, :, None] * val_second.T[:, None, :])
            .astype(jnp.bfloat16)
            .reshape(mu_dev, nval * nval)
        )
        exc_first = full_exc[slot_index].reshape(nval, ncon, nexc)
        exc_second = full_exc[slots + slot_index].reshape(nval, ncon, nexc)
        lower = 0
        upper = lower + PTS_BLK
        kernel = jnp.dot(screened, rho_val, preferred_element_type=jnp.float32)
        kernel = kernel.astype(jnp.bfloat16).reshape(ncon, ncon, nval, nval)
        ahead = jnp.einsum("cdvw,wde->vce", kernel, exc_second, preferred_element_type=jnp.float32)
        back = jnp.einsum("cdvw,vce->wde", kernel, exc_first, preferred_element_type=jnp.float32)
        ahead_list.append(ahead.reshape(nval * ncon, nexc))
        back_list.append(back.reshape(nval * ncon, nexc))
    ahead_all = jnp.stack(ahead_list)[None]
    back_all = jnp.stack(back_list)[None]
    ahead_own, back_own = in_one_piece_2((ahead_all, back_all), "scr", 2, 0)
    live = (jnp.arange(slots, dtype=jnp.int32) < pair_count[0]).astype(jnp.float32)[
        None, :, None, None
    ]
    return (ahead_own * live, back_own * live)


def solution(mesh):
    return jax.shard_map(
        body,
        mesh=mesh,
        in_specs=(
            P("kgrp", None, "scr"),
            P("kgrp", None, "scr"),
            P("kgrp", "scr", None),
            P("kgrp", None, "scr"),
            P("kgrp"),
            P("kgrp", None),
            P("kgrp", None),
        ),
        out_specs=(P("kgrp", None, "scr", None), P("kgrp", None, "scr", None)),
        check_vma=False,
    )
```

profile of v0, /device:TPU:1, one launch (start us, length us, event | category | flops | bytes accessed | tf_op | source)
XLA Modules:
  0.0 220.1 jit_solution(17392317176469980804)
XLA Ops:
  7.2 0.8 copy.49
  8.1 0.7 copy_bitcast_fusion.5
  9.5 0.7 pad_add_fusion
  10.3 101.1 %all-gather.4.cloned.1.call-done = bf16[64,1,9216]{2,1,0:T(2,128)(2,1)} async-done(((bf16[1,1,9216]{2,1,0:T(2,128)(2,1)}), bf16[64,1,9216]{2,1,0:T(2,128)(2,1)}) %all-gather.4.cloned.1.call-update) | async-done | bytes 1179664 | tf_op jit(solution)/shard_map/all_gather | solution.py:16
  111.3 2.0 copy.100
  114.1 23.6 %all-gather = bf16[327680]{0:T(1024)(128)(2,1)S(1)} all-gather(bf16[20480]{0:T(1024)(128)(2,1)S(1)} %pad_maximum_fusion), channel_id=2, replica_groups=mesh['kgrp'=64,'scr'=16] {'scr'}, dimensions={0}, use_global_device_ids=true | all-gather | bytes 696320 | tf_op jit(solution)/shard_map/all_gather | solution.py:29
  138.2 0.7 fusion.37
  141.5 1.2 convolution_add_fusion.4
  143.1 2.1 convolution_convert_fusion.3
  145.2 8.1 %reshape.224 = bf16[32,32,32,32]{3,2,1,0:T(8,128)(2,1)} reshape(bf16[1024,1024]{1,0:T(8,128)(2,1)S(1)} %convolution_convert_fusion.3) | data formatting | bytes 4194304 | tf_op jit(solution)/shard_map/reshape | solution.py:117
  153.3 0.8 reshape.222
  154.1 0.9 fusion.36
  155.4 5.8 %convolution_bitcast_fusion.3 = f32[32,32,16]{0,2,1:T(8,128)S(1)} fusion(bf16[32,32,32,32]{3,2,1,0:T(8,128)(2,1)} %reshape.224, bf16[32,32,16]{0,2,1:T(8,128)(2,1)S(1)} %copy.53), kind=kOutput, calls=%fused_computation.24 | convolution fusion | flops 33554432 | bytes 2195456 | tf_op jit(solution)/shard_map/cdvw,wde->vce/dot_general | solution.py:118
  161.8 4.9 %convolution_bitcast_fusion.1 = f32[32,32,16]{0,2,1:T(8,128)S(1)} fusion(bf16[32,32,32,32]{3,2,1,0:T(8,128)(2,1)} %reshape.224, bf16[32,32,16]{0,2,1:T(8,128)(2,1)S(1)} %copy.61), kind=kOutput, calls=%fused_computation.22 | convolution fusion | flops 33554432 | bytes 2195456 | tf_op jit(solution)/shard_map/cdvw,vce->wde/dot_general | solution.py:119
  166.8 0.8 stack.17
  169.5 1.2 convolution_add_fusion.1
  171.1 2.1 convolution_convert_fusion.2
  173.2 7.9 %reshape.225 = bf16[32,32,32,32]{3,2,1,0:T(8,128)(2,1)} reshape(bf16[1024,1024]{1,0:T(8,128)(2,1)S(1)} %convolution_convert_fusion.2) | data formatting | bytes 4194304 | tf_op jit(solution)/shard_map/reshape | solution.py:117
  181.5 5.8 %convolution_bitcast_fusion.2 = f32[32,32,16]{0,2,1:T(8,128)S(1)} fusion(bf16[32,32,32,32]{3,2,1,0:T(8,128)(2,1)} %reshape.225, bf16[32,32,16]{0,2,1:T(8,128)(2,1)S(1)} %copy.58), kind=kOutput, calls=%fused_computation.23 | convolution fusion | flops 33554432 | bytes 2195456 | tf_op jit(solution)/shard_map/cdvw,wde->vce/dot_general | solution.py:118
  187.9 4.9 %convolution_bitcast_fusion = f32[32,32,16]{0,2,1:T(8,128)S(1)} fusion(bf16[32,32,32,32]{3,2,1,0:T(8,128)(2,1)} %reshape.225, bf16[32,32,16]{0,2,1:T(8,128)(2,1)S(1)} %copy.65), kind=kOutput, calls=%fused_computation.21 | convolution fusion | flops 33554432 | bytes 2195456 | tf_op jit(solution)/shard_map/cdvw,vce->wde/dot_general | solution.py:119
  193.3 1.0 reshape.241
  194.3 4.6 %all-to-all-start = ((f32[16,1,4096]{2,1,0:T(1,128)}), f32[16,1,4096]{2,1,0:T(1,128)S(1)}, u32[]{:S(2)}, u32[]{:S(2)}) async-start(f32[16,1,4096]{2,1,0:T(1,128)} %reshape.241), calls=%async_computation | async-start | bytes 524288 | tf_op jit(solution)/shard_map/all_to_all | solution.py:45
  199.6 10.9 %all-to-all-done = f32[16,1,4096]{2,1,0:T(1,128)S(1)} async-done(((f32[16,1,4096]{2,1,0:T(1,128)}), f32[16,1,4096]{2,1,0:T(1,128)S(1)}, u32[]{:S(2)}, u32[]{:S(2)}) %all-to-all-start) | async-done | bytes 262176 | tf_op jit(solution)/shard_map/all_to_all | solution.py:45
  211.0 1.3 reduce
  (78 shorter events, 10.8 us)
Async XLA Ops:
  7.2 104.2 %all-gather.4.cloned.1.call-start = ((), (), s32[]{:S(2)}) async-start(), calls=%async_computation.1 | async-start | bytes 2396160 | tf_op jit(solution)/shard_map/all_gather | solution.py:16
  138.0 1.0 copy-start
  138.2 1.9 copy-start.1
  145.2 8.1 %slice-start = ((bf16[16,20480]{1,0:T(8,128)(2,1)}), bf16[16,4096]{1,0:T(8,128)(2,1)S(1)}, s32[]{:S(2)}) async-start(bf16[16,20480]{1,0:T(8,128)(2,1)} %copy-done), calls=%async_computation.2 | async-start | bytes 262144 | tf_op jit(solution)/shard_map/slice | solution.py:31
  161.8 5.8 %copy-start.7 = (bf16[1,32,16,128]{3,1,0,2:T(8,128)(2,1)S(1)}, bf16[1,32,16,128]{3,1,0,2:T(8,128)(2,1)}, u32[]{:S(2)}) copy-start(bf16[1,32,16,128]{3,1,0,2:T(8,128)(2,1)} %get-tuple-element.8) | copy-start | bytes 393220
  161.8 5.9 %copy-start.6 = (bf16[1,32,16,128]{3,1,0,2:T(8,128)(2,1)S(1)}, bf16[1,32,16,128]{3,1,0,2:T(8,128)(2,1)}, u32[]{:S(2)}) copy-start(bf16[1,32,16,128]{3,1,0,2:T(8,128)(2,1)} %get-tuple-element.7) | copy-start | bytes 393220
  166.6 1.5 copy-start.2
  169.2 1.8 copy-start.8
  173.2 8.0 %copy-start.4 = (bf16[1,16,64,16]{3,2,0,1:T(8,128)(2,1)S(1)}, bf16[1,16,64,16]{3,2,0,1:T(8,128)(2,1)}, u32[]{:S(2)}) copy-start(bf16[1,16,64,16]{3,2,0,1:T(8,128)(2,1)} %get-tuple-element.5) | copy-start | bytes 98308
  181.5 6.1 %copy-start.3 = (bf16[1,16,64,16]{3,2,0,1:T(8,128)(2,1)S(1)}, bf16[1,16,64,16]{3,2,0,1:T(8,128)(2,1)}, u32[]{:S(2)}) copy-start(bf16[1,16,64,16]{3,2,0,1:T(8,128)(2,1)} %get-tuple-element.3) | copy-start | bytes 98308
  187.9 5.1 %copy-start.5 = (f32[1,1,16,64,16]{3,2,4,1,0:T(8,128)S(1)}, f32[1,1,16,64,16]{3,2,4,1,0:T(8,128)}, u32[]{:S(2)}) copy-start(f32[1,1,16,64,16]{3,2,4,1,0:T(8,128)} %stack.17) | copy-start | bytes 196612
  194.3 16.2 %all-to-all-start = ((f32[16,1,4096]{2,1,0:T(1,128)}), f32[16,1,4096]{2,1,0:T(1,128)S(1)}, u32[]{:S(2)}, u32[]{:S(2)}) async-start(f32[16,1,4096]{2,1,0:T(1,128)} %reshape.241), calls=%async_computation | async-start | bytes 524288 | tf_op jit(solution)/shard_map/all_to_all | solution.py:45
Sparse Core Ops, SparseCore 0:
  12.2 99.0 all-gather.3
where the time goes:
time: 221 us; the launch traced here: 220 us
  waiting for transfers between devices  112 us (51%)
  matrix products  30.4 us (14%)
  local copies, waits for them, and re-layouts  28 us (13%)
  blocking collectives  23.6 us (11%)
  between operations  15.1 us (7%)
  other arithmetic  6.3 us (3%)
  starting transfers between devices  4.66 us (2%)
    all_gather x1, waiting for transfers between devices, in_one_piece(): out = lax.all_gather(both, axis, axis=dim, tiled=True)  101 us
    all_gather x1, blocking collectives, gather_together(): lines, at, done = (lax.all_gather(vector, axis), 0, [])  23.6 us
    reshape x2, local copies, waits for them, and re-layouts, body(): kernel = kernel.astype(jnp.bfloat16).reshape(ncon, ncon, nval, nval)  16.1 us
    dot_general x2, matrix products, body(): jnp.einsum('cdvw,wde->vce', kernel, exc_second, preferred_element_type=jn...  11.6 us
    all_to_all x1, waiting for transfers between devices, sent_and_summed(): lax.all_to_all(tiles, axis, split_axis=0, concat_axis=0, tiled=True)  10.9 us
    dot_general x2, matrix products, body(): jnp.einsum('cdvw,vce->wde', kernel, exc_first, preferred_element_type=jnp...  9.75 us
    all_to_all x1, starting transfers between devices, sent_and_summed(): lax.all_to_all(tiles, axis, split_axis=0, concat_axis=0, tiled=True)  4.62 us
  transfers between devices with their start and end apart: 2, of which 2 were waited for; matrix products, arithmetic and copies ran while one was open for 0% of the time, Pallas kernels for 0%

commit v1 on v0

v1 whole, which is shorter than its diff:
```python
import math

import jax
import jax.numpy as jnp
from jax import lax
from jax.experimental import pallas as pl
from jax.experimental.pallas import tpu as pltpu
from jax.sharding import PartitionSpec as P

MESH = pl.DeviceIdType.MESH
BF16 = jnp.bfloat16
F32 = jnp.float32

NB = 32
NE = 16
PT = 128
DE = NB * NE


def ring(n):
    right, left = n // 2, (n - 1) // 2
    out = []
    for s in range(1, right + 1):
        out.append(("R", s))
        if s <= left:
            out.append(("L", s))
    return out


def slot_of(kind, s):
    return 2 * s - 1 if kind == "R" else 2 * s


def build(nx, nz, ny):
    steps_x, steps_z, steps_y = ring(nx), ring(nz), ring(ny)
    right_x, right_z = nx // 2, nz // 2

    def chunks(n):
        edges = sorted({0, min(3, n), min(5, n), n})
        return [(a, b) for a, b in zip(edges[:-1], edges[1:])]

    n_sems = 320

    def kernel(
        val_ref, con_ref, exc_ref, scr_ref, cnt_ref, first_ref, second_ref,
        fwd_ref, back_ref,
        W, GCA, GCB, GVA, GVB, GE, CB, SC, EB, SE, VB, SV, own_e,
        xt, xr, S, E32, Y1, Y2, V32, Zf, Zb, T32, SB, RB, O32,
        send_sem, recv_sem, local_sem,
    ):
        g = lax.axis_index("kgrp")
        sc = lax.axis_index("scr")
        x = lax.div(g, nz)
        z = lax.rem(g, nz)
        y = lax.div(sc, 2)
        core = lax.rem(sc, 2)
        other = 1 - core

        def at_x(d):
            return (lax.rem(x + d + nx, nx) * nz + z, sc)

        def at_z(d):
            return (x * nz + lax.rem(z + d + nz, nz), sc)

        def at_y(d):
            return (g, lax.rem(y + d + ny, ny) * 2 + core)

        partner = (g, y * 2 + other)

        peers = [partner]
        for n, at in ((nx, at_x), (nz, at_z), (ny, at_y)):
            if n > 2:
                peers += [at(1), at(-1)]
            elif n == 2:
                peers += [at(1)]
        barrier = pltpu.get_barrier_semaphore()
        for peer in peers:
            pl.semaphore_signal(barrier, inc=1, device_id=peer, device_id_type=MESH)
        pl.semaphore_wait(barrier, len(peers))

        started = []
        count = [0]

        def send(src, dst, to):
            k = count[0]
            count[0] += 1
            copy = pltpu.make_async_remote_copy(
                src_ref=src, dst_ref=dst, send_sem=send_sem.at[k], recv_sem=recv_sem.at[k],
                device_id=to, device_id_type=MESH,
            )
            copy.start()
            started.append(copy)
            return copy

        class Ring:
            def __init__(self, n, at, view, own=None):
                self.n, self.at, self.view = n, at, view
                self.right, self.left = n // 2, (n - 1) // 2
                self.flight = {}
                self.own = own

            def begin(self):
                for kind, d, last in (("R", 1, self.right), ("L", -1, self.left)):
                    if last >= 1:
                        src = self.view(0) if self.own is None else self.own
                        self.flight[kind, 1] = send(src, self.view(slot_of(kind, 1)), self.at(d))

            def step(self, s):
                for kind, d, last in (("R", 1, self.right), ("L", -1, self.left)):
                    if s <= last:
                        self.flight[kind, s].wait_recv()
                        if s + 1 <= last:
                            self.flight[kind, s + 1] = send(
                                self.view(slot_of(kind, s)), self.view(slot_of(kind, s + 1)), self.at(d)
                            )

        ca1 = Ring(nx, at_x, lambda k: GCA.at[0, k], con_ref.at[pl.ds(0, 16)])
        cb1 = Ring(nz, at_z, lambda k: GCB.at[0, k], con_ref.at[pl.ds(16, 16)])
        ca1.begin()
        cb1.begin()
        w_here = pltpu.make_async_copy(scr_ref, W.at[core], local_sem)
        w_here.start()
        xt[...] = jnp.zeros_like(xt)
        xr[...] = jnp.zeros_like(xr)
        xt[:, 0:64] = exc_ref[...].astype(F32)
        xr[:, 0:NE] = xt[...].T[:, 0:NE]
        packed = xr[pl.ds(0, 8, stride=8), :]
        for k in range(1, 8):
            packed = packed + pltpu.roll(xr[pl.ds(k, 8, stride=8), :], NE * k, 1)
        own_e[...] = packed.astype(BF16)
        GE[0, 0] = packed.astype(BF16)
        GCA[0, 0] = con_ref[0:16, :]
        GCB[0, 0] = con_ref[16:32, :]
        GVA[0, 0] = val_ref[0:16, :]
        GVB[0, 0] = val_ref[16:32, :]
        va1 = Ring(nx, at_x, lambda k: GVA.at[0, k], val_ref.at[pl.ds(0, 16)])
        vb1 = Ring(nz, at_z, lambda k: GVB.at[0, k], val_ref.at[pl.ds(16, 16)])
        ex1 = Ring(nx, at_x, lambda k: GE.at[0, k], own_e)
        ex1.begin()
        va1.begin()
        vb1.begin()
        w_there = send(scr_ref, W.at[core], partner)

        def second(buf, n_first, n, at, lo, hi):
            return Ring(n, at, lambda k: buf.at[k, pl.ds(lo, hi - lo)])

        con_rings = []
        for lo, hi in chunks(nx):
            con_rings.append((hi // 2, second(GCA, nx, nz, at_z, lo, hi)))
        for lo, hi in chunks(nz):
            con_rings.append((hi // 2, second(GCB, nz, nx, at_x, lo, hi)))
        ex2 = second(GE, nx, nz, at_z, 0, nx)
        va2 = second(GVA, nx, nz, at_z, 0, nx)
        vb2 = second(GVB, nz, nx, at_x, 0, nz)
        half = max(nx, nz) // 2
        for t in range(1, 2 * half + 1):
            ca1.step(t)
            cb1.step(t)
            for ready, r in con_rings:
                if t == ready:
                    r.begin()
                elif t > ready:
                    r.step(t - ready)
            ex1.step(t)
            if t == half:
                ex2.begin()
            elif t > half:
                ex2.step(t - half)
            va1.step(t)
            vb1.step(t)
            if t == half:
                va2.begin()
                vb2.begin()

        def slots(k):
            kx = lax.div(k, nz)
            kz = lax.rem(k, nz)
            rx = lax.rem(x - kx + nx, nx)
            rz = lax.rem(z - kz + nz, nz)
            sx = jnp.where(rx <= right_x, jnp.maximum(2 * rx - 1, 0), 2 * (nx - rx))
            sz = jnp.where(rz <= right_z, jnp.maximum(2 * rz - 1, 0), 2 * (nz - rz))
            return sx, sz

        chosen = {}
        for name, p in (("own", core), ("other", other)):
            for role, ref in ((0, first_ref), (1, second_ref)):
                chosen[name, role] = slots(ref[0, p])

        for role in (0, 1):
            sx, sz = chosen["other", role]
            SC[role, 0:16, :] = GCA[sz, sx]
            SC[role, 16:32, :] = GCB[sx, sz]
            sx, sz = chosen["own", role]
            CB[0, core, role, 0:16, :] = GCA[sz, sx]
            CB[0, core, role, 16:32, :] = GCB[sx, sz]
        for role in (0, 1):
            sx, sz = chosen["other", role]
            SE[role] = GE[sz, sx]
            sx, sz = chosen["own", role]
            EB[0, core, role] = GE[sz, sx]
        pc = send(SC, CB.at[0, core], partner)
        y_own = Ring(ny, at_y, lambda k: CB.at[k, core])
        y_oth = Ring(ny, at_y, lambda k: CB.at[k, other])
        y_exc = Ring(ny, at_y, lambda k: EB.at[k])
        y_own.begin()
        pe = send(SE, EB.at[0, core], partner)
        pc.wait_recv()
        y_oth.begin()
        pe.wait_recv()
        y_exc.begin()
        w_here.wait()
        w_there.wait_recv()

        def y_from(k):
            if k == 0:
                return y
            s = (k + 1) // 2
            return lax.rem(y - s + ny, ny) if k % 2 == 1 else lax.rem(y + s, ny)

        def block(k):
            row = pl.multiple_of(y_from(k) * (2 * PT), 2 * PT)
            w = jnp.concatenate([W[0, pl.ds(row, 2 * PT), :], W[1, pl.ds(row, 2 * PT), :]], axis=1)
            c1 = jnp.concatenate([CB[k, 0, 0], CB[k, 1, 0]], axis=1).astype(F32)
            c2 = jnp.concatenate([CB[k, 0, 1], CB[k, 1, 1]], axis=1).astype(F32)
            for b in range(4):
                rho = jnp.concatenate(
                    [(c1[c : c + 1, :] * c2).astype(BF16) for c in range(8 * b, 8 * b + 8)], axis=0
                )
                part = jnp.dot(rho, w, preferred_element_type=F32)
                for lane in range(2):
                    piece = part[:, 128 * lane : 128 * lane + 128]
                    if k == 0:
                        S[lane, pl.ds(256 * b, 256), :] = piece
                    else:
                        S[lane, pl.ds(256 * b, 256), :] += piece

        block(0)
        for t in range(1, max(half, ny // 2) + 1):
            y_own.step(t)
            y_oth.step(t)
            y_exc.step(t)
            va2.step(t)
            vb2.step(t)
            for kind, s in steps_y:
                if s == t:
                    block(slot_of(kind, s))

        for role in (0, 1):
            sx, sz = chosen["other", role]
            SV[role, 0:16, :] = GVA[sz, sx]
            SV[role, 16:32, :] = GVB[sx, sz]
            sx, sz = chosen["own", role]
            VB[core, role, 0:16, :] = GVA[sz, sx]
            VB[core, role, 16:32, :] = GVB[sx, sz]
        pv = send(SV, VB.at[core], partner)

        for k in range(ny):
            for c in range(2):
                row = pl.multiple_of((y_from(k) * 2 + c) * 8, 8)
                for role in (0, 1):
                    E32[role, pl.ds(row, 8), :] = EB[k, c, role].astype(F32)
        pv.wait_recv()
        vals = [jnp.concatenate([VB[0, role], VB[1, role]], axis=1) for role in (0, 1)]
        nw = 4 * ny
        for role, out in ((0, Y1), (1, Y2)):
            for lane in range(2):
                V32[role, lane] = VB[lane, role].astype(F32)
            for q in range(4):
                eq = E32[role, pl.ds(q, nw, stride=4), :].astype(BF16)
                out[pl.ds(q * 128, 128), :] = lax.dot_general(
                    eq, vals[role][0:nw], (((0,), (0,)), ((), ())), preferred_element_type=F32
                )
        Zb[...] = jnp.zeros_like(Zb)

        def z_block(i, carry):
            for lane in range(2):
                cols = pl.ds(lane * 128, 128)
                y1 = [Y1[pl.ds(pl.multiple_of((i * 8 + c) * NE, NE), NE), cols] for c in range(8)]

                def over_d(d, acc):
                    at = pl.multiple_of(d * NE, NE)
                    y2 = Y2[pl.ds(at, NE), cols]
                    mirror = pl.multiple_of((d + 7 - 2 * lax.rem(d, 8)) * NE, NE)
                    zb = Zb[pl.ds(mirror, NE), cols]
                    new = []
                    for c in range(8):
                        s = S[lane, pl.ds((i * 8 + c) * NB + d, 1), :]
                        new.append(acc[c] + s * y2)
                        zb = zb + s * y1[c]
                    Zb[pl.ds(mirror, NE), cols] = zb
                    return tuple(new)

                zero = tuple(jnp.zeros((NE, 128), F32) for c in range(8))
                acc = lax.fori_loop(0, NB, over_d, zero)
                for c in range(8):
                    Zf[pl.ds(pl.multiple_of((i * 8 + 7 - c) * NE, NE), NE), cols] = acc[c]
            return carry

        lax.fori_loop(0, 4, z_block, 0)

        for fb, Z, role in ((0, Zf, 0), (1, Zb, 1)):
            v = jnp.concatenate(
                [
                    jnp.concatenate(
                        [V32[role, lane, pl.ds(i, 16, stride=2), :] for lane in range(2)], axis=1
                    )
                    for i in range(2)
                ],
                axis=0,
            ).astype(BF16)
            for h in range(4):
                f = lax.dot_general(
                    v, Z[pl.ds(h * 128, 128), :].astype(BF16), (((1,), (1,)), ((), ())),
                    preferred_element_type=F32,
                )
                for i in range(2):
                    T32[pl.ds(fb * 8 + h * 2 + i, 16, stride=16), :] = f[16 * i : 16 * i + 16, :]
        n_scr = 2 * ny
        for s in range(n_scr):
            SB[s] = T32[pl.ds(16 * s, 16), :].astype(BF16)
        RB[core, 0] = SB[sc]
        sums = []
        for d in range(ny):
            for c, cc in ((0, core), (1, other)):
                if d == 0 and c == 0:
                    continue
                yy = lax.rem(y + d, ny)
                to = yy * 2 + cc
                sums.append(send(SB.at[to], RB.at[core, d], (g, to)))
        for copy in started:
            copy.wait_send()
        for copy in sums:
            copy.wait_recv()
        O32[...] = jnp.zeros_like(O32)
        for p in range(2):
            live = jnp.where(p < cnt_ref[0], 1.0, 0.0).astype(F32)
            tot = RB[p, 0].astype(F32)
            for d in range(1, ny):
                tot = tot + RB[p, d].astype(F32)
            tot = tot * live
            for fb, out in ((0, fwd_ref), (1, back_ref)):
                for i in range(2):
                    for h in range(4):
                        r = fb * 8 + h * 2 + i
                        row = jnp.broadcast_to(tot[r : r + 1, :], (8, 128))
                        O32[pl.ds(i * 32 + h * 8, 8), :] = pltpu.roll(
                            pltpu.roll(row, NE, 1), 0, 1, stride=NE, stride_axis=0
                        )
                out[p] = O32[...].T[0:NE, 0:64]

    def run(wave_val, wave_con, excite, screening, pair_count, pair_kpoint, pair_partner):
        vmem = pl.BlockSpec(memory_space=pltpu.VMEM)
        smem = pl.BlockSpec(memory_space=pltpu.SMEM)
        n_mu = 2 * PT * ny
        shape = jax.ShapeDtypeStruct((2, NE, 64), F32)
        V = pltpu.VMEM
        fwd, back = pl.pallas_call(
            kernel,
            out_shape=(shape, shape),
            in_specs=[vmem, vmem, vmem, pl.BlockSpec(memory_space=pl.ANY), smem, smem, smem],
            out_specs=(vmem, vmem),
            scratch_shapes=[
                V((2, n_mu, PT), BF16),
                V((nz, nx, 16, PT), BF16), V((nx, nz, 16, PT), BF16),
                V((nz, nx, 16, PT), BF16), V((nx, nz, 16, PT), BF16),
                V((nz, nx, 8, PT), BF16),
                V((ny, 2, 2, NB, PT), BF16), V((2, NB, PT), BF16),
                V((ny, 2, 2, 8, PT), BF16), V((2, 8, PT), BF16),
                V((2, 2, NB, PT), BF16), V((2, NB, PT), BF16),
                V((8, PT), BF16),
                V((16, 128), F32), V((128, 128), F32),
                V((2, NB * NB, PT), F32),
                V((2, 16 * ny, 128), F32),
                V((DE, 2 * PT), F32), V((DE, 2 * PT), F32),
                V((2, 2, NB, PT), F32),
                V((DE, 2 * PT), F32), V((DE, 2 * PT), F32),
                V((256, 128), F32), V((16, 16, 128), BF16), V((2, ny, 16, 128), BF16),
                V((128, 128), F32),
                pltpu.SemaphoreType.DMA((n_sems,)), pltpu.SemaphoreType.DMA((n_sems,)),
                pltpu.SemaphoreType.DMA,
            ],
            compiler_params=pltpu.CompilerParams(
                collective_id=0, has_side_effects=True, vmem_limit_bytes=32 * 1024 * 1024
            ),
        )(
            wave_val[0], wave_con[0], jnp.transpose(excite[0]), screening[0],
            pair_count, pair_kpoint, pair_partner,
        )
        return jnp.swapaxes(fwd, 1, 2)[None], jnp.swapaxes(back, 1, 2)[None]

    return run


def solution(mesh, sides=None):
    side = math.isqrt(mesh.shape["kgrp"])
    nx, nz = sides or (side, side)
    return jax.shard_map(
        build(nx, nz, mesh.shape["scr"] // 2),
        mesh=mesh,
        in_specs=(
            P("kgrp", None, "scr"),
            P("kgrp", None, "scr"),
            P("kgrp", "scr", None),
            P("kgrp", None, "scr"),
            P("kgrp"),
            P("kgrp", None),
            P("kgrp", None),
        ),
        out_specs=(P("kgrp", None, "scr", None), P("kgrp", None, "scr", None)),
        check_vma=False,
    )
```

time: 221 us -> 85.7 us (0.39)
  waiting for transfers between devices: 112 us -> 0 us
  Pallas kernels: 0 us -> 79.8 us
  matrix products: 30.4 us -> 0 us
  local copies, waits for them, and re-layouts: 28 us -> 4.29 us
  blocking collectives: 23.6 us -> 0 us
  between operations: 15.1 us -> 1.33 us
  other arithmetic: 6.3 us -> 0 us
  starting transfers between devices: 4.66 us -> 0 us
    all_gather x1 -> x0, waiting for transfers between devices: 101 us -> none  [in_one_piece(): out = lax.all_gather(both, axis, axis=dim, tiled=True)]
    pallas_call x0 -> x1, Pallas kernels: none -> 79.8 us  [run(): pl.pallas_call(kernel, out_shape=(shape, shape), in_specs=[vmem, vmem, vm...]
    dot_general x15 -> x0, matrix products: 30.4 us -> none  [the longest x2 11.6 us: body(): jnp.einsum('cdvw,wde->vce', kernel, exc_second, preferred_element_type=jn...]
    all_gather x1 -> x0, blocking collectives: 23.6 us -> none  [gather_together(): lines, at, done = (lax.all_gather(vector, axis), 0, [])]
    reshape x5 -> x0, local copies, waits for them, and re-layouts: 17.7 us -> none  [the longest x2 16.1 us: body(): kernel = kernel.astype(jnp.bfloat16).reshape(ncon, ncon, nval, nval)]
    all_to_all x1 -> x0, waiting for transfers between devices: 10.9 us -> none  [sent_and_summed(): lax.all_to_all(tiles, axis, split_axis=0, concat_axis=0, tiled=True)]
    all_to_all x1 -> x0, starting transfers between devices: 4.62 us -> none  [sent_and_summed(): lax.all_to_all(tiles, axis, split_axis=0, concat_axis=0, tiled=True)]
    another operation x8 -> x0, local copies, waits for them, and re-layouts: 2.36 us -> none  [the longest x2 0.85 us: body(): back_all = jnp.stack(back_list)[None]]
  transfers between devices with their start and end apart: 2 -> 0, of which waited for: 2 -> 0; matrix products, arithmetic and copies ran while one was open for 0% -> 0% of each run, Pallas kernels for 0% -> 0%
where the time goes in v1:
time: 85.7 us; the launch traced here: 85.4 us
  Pallas kernels  79.8 us (93%)
  local copies, waits for them, and re-layouts  4.29 us (5%)
  between operations  1.33 us (2%)
    pallas_call x1, Pallas kernels, run(): pl.pallas_call(kernel, out_shape=(shape, shape), in_specs=[vmem, vmem, vm...  79.8 us
    unnamed x14, local copies, waits for them, and re-layouts  4.29 us

profile of v1, /device:TPU:1, one launch (start us, length us, event | category | flops | bytes accessed | tf_op | source)
XLA Modules:
  0.0 85.4 jit_solution(2335840898752492144)
XLA Ops:
  0.6 0.0 copy-start.1
  1.3 0.0 copy-start.4
  1.3 0.0 copy-start.5
  1.3 0.0 copy-done.1
  1.3 0.6 copy-done.4
  2.0 0.0 copy-done.5
  2.0 0.0 copy-start
  2.0 1.0 %copy-done = bf16[1,2048,128]{2,1,0:T(8,128)(2,1)S(1)} copy-done((bf16[1,2048,128]{2,1,0:T(8,128)(2,1)S(1)}, bf16[1,2048,128]{2,1,0:T(8,128)(2,1)}, u32[]{:S(2)}) %copy-start) | copy-done | bytes 524312
  3.0 0.0 copy-start.2
  3.0 0.7 copy-done.2
  3.7 0.0 copy-start.3
  3.7 0.7 copy-done.3
  4.4 79.8 %shard_map.86 = (f32[2,16,64]{2,1,0:T(8,128)S(1)}, f32[2,16,64]{2,1,0:T(8,128)S(1)}) custom-call(bf16[32,128]{1,0:T(8,128)(2,1)S(1)} %bitcast.15, bf16[32,128]{1,0:T(8,128)(2,1)S(1)} %bitcast.16, bf16[16,64]{1,0:T(8,128)(2,1)S(1)} %bitcast.17, bf16[2048,128]{1,0:T(8,128)(2,1)S(1)} %bitcast.12, s32[1]{0:T(128)S(6)} %copy.11.cnt_ref, s32[1,2]{1,0:T(1,128)S(1)} %copy-done.4, ...), custom_call_target="tpu_custom_call" | custom-call | tf_op jit(solution)/shard_map/pallas_call | solution.py:357
  84.2 0.6 copy.12
  84.8 0.6 copy.13
Async XLA Ops:
  0.6 0.7 copy-start.1
  1.3 0.7 copy-start.4
  1.3 0.7 copy-start.5
  2.0 1.0 %copy-start = (bf16[1,2048,128]{2,1,0:T(8,128)(2,1)S(1)}, bf16[1,2048,128]{2,1,0:T(8,128)(2,1)}, u32[]{:S(2)}) copy-start(bf16[1,2048,128]{2,1,0:T(8,128)(2,1)} %param.10) | copy-start | bytes 1572868
  3.0 0.7 copy-start.2
  3.7 0.7 copy-start.3

commit v2 on v1

v2 whole, which is shorter than its diff:
```python
import math

import jax
import jax.numpy as jnp
from jax import lax
from jax.experimental import pallas as pl
from jax.experimental.pallas import tpu as pltpu
from jax.sharding import PartitionSpec as P

MESH = pl.DeviceIdType.MESH
BF16 = jnp.bfloat16
F32 = jnp.float32

NB = 32
NE = 16
PT = 128
DE = NB * NE


def build(nx, nz, ny):
    n_scr = 2 * ny
    n_groups = 14 + ny

    def kernel(
        val_ref, con_ref, exc_ref, scr_ref, cnt_ref, first_ref, second_ref,
        fwd_ref, back_ref,
        W, con_v, val_v, exc_v, own_i, IX, IZ, SX, SZ,
        GCA, GCB, GVA, GVB, GE, PCA, PCB, PVA, PVB, PE, RCA, RCB, RVA, RVB, RE,
        CB, EB, xt, xr, S, E32, Y1, Y2, V32, Zf, Zb, T32, SB, RB, O32,
        send_sem, recv_sem, local_sem,
    ):
        g = lax.axis_index("kgrp")
        sc = lax.axis_index("scr")
        x = lax.div(g, nz)
        z = lax.rem(g, nz)
        y = lax.div(sc, 2)
        core = lax.rem(sc, 2)
        other = 1 - core

        def at_x(d, c):
            return (lax.rem(x + d, nx) * nz + z, y * 2 + c)

        def at_z(d, c):
            return (x * nz + lax.rem(z + d, nz), y * 2 + c)

        def at_y(d, c):
            return (g, lax.rem(y + d, ny) * 2 + c)

        def far_first(n):
            return sorted(range(1, n), key=lambda d: -min(d, n - d))

        loads = [
            pltpu.make_async_copy(src, dst, local_sem.at[i])
            for i, (src, dst) in enumerate(
                ((con_ref, con_v), (exc_ref, exc_v), (val_ref, val_v), (scr_ref, W.at[core]))
            )
        ]
        for load in loads:
            load.start()
        peers = [at_x(d, c) for d in far_first(nx) for c in (core, other)]
        peers += [at_z(d, c) for d in far_first(nz) for c in (core, other)]
        peers += [at_y(d, core) for d in far_first(ny)] + [at_y(0, other)]
        barrier = pltpu.get_barrier_semaphore()
        for peer in peers:
            pl.semaphore_signal(barrier, inc=1, device_id=peer, device_id_type=MESH)

        groups = {}

        def send(name, src, dst, to):
            k = groups.setdefault(name, len(groups))
            pltpu.make_async_remote_copy(
                src_ref=src, dst_ref=dst, send_sem=send_sem.at[k], recv_sem=recv_sem.at[k],
                device_id=to, device_id_type=MESH,
            ).start()

        def taken(name, sems, like):
            pltpu.make_async_copy(like, like, sems.at[groups[name]]).wait()

        lane = lax.broadcasted_iota(jnp.int32, (1, 128), 1)
        row = jnp.zeros((1, 128), jnp.int32)
        for i, ref in ((0, first_ref), (1, second_ref)):
            for p in range(2):
                row = jnp.where(lane == 2 * i + p, ref[0, p], row)
        own_i[...] = row
        IX[0] = row
        IZ[0] = row
        loads[0].wait()
        GCA[0] = con_v[0:16, :]
        GCB[0] = con_v[16:32, :]
        xt[...] = jnp.zeros_like(xt)
        xr[...] = jnp.zeros_like(xr)
        loads[1].wait()
        xt[:, 0:64] = exc_v[...].astype(F32)
        xr[:, 0:NE] = xt[...].T[:, 0:NE]
        packed = xr[pl.ds(0, 8, stride=8), :]
        for k in range(1, 8):
            packed = packed + pltpu.roll(xr[pl.ds(k, 8, stride=8), :], NE * k, 1)
        GE[0] = packed.astype(BF16)
        loads[2].wait()
        GVA[0] = val_v[0:16, :]
        GVB[0] = val_v[16:32, :]
        pl.semaphore_wait(barrier, len(peers))

        for d in far_first(nx):
            send("ix", own_i, IX.at[d], at_x(d, core))
        for d in far_first(nz):
            send("iz", own_i, IZ.at[d], at_z(d, core))
        for d in far_first(nx):
            send("ca1", con_v.at[pl.ds(0, 16)], GCA.at[d], at_x(d, core))
        for d in far_first(nz):
            send("cb1", con_v.at[pl.ds(16, 16)], GCB.at[d], at_z(d, core))
        for d in far_first(nx):
            send("e1", GE.at[0], GE.at[d], at_x(d, core))
        for d in far_first(nx):
            send("va1", val_v.at[pl.ds(0, 16)], GVA.at[d], at_x(d, core))
        for d in far_first(nz):
            send("vb1", val_v.at[pl.ds(16, 16)], GVB.at[d], at_z(d, core))
        send("w", scr_ref, W.at[core], at_y(0, other))

        taken("ix", recv_sem, IX.at[pl.ds(0, nx - 1)])
        ix_down = pltpu.make_async_copy(IX, SX, local_sem.at[0])
        ix_down.start()
        taken("iz", recv_sem, IZ.at[pl.ds(0, nz - 1)])
        iz_down = pltpu.make_async_copy(IZ, SZ, local_sem.at[1])
        iz_down.start()

        def place(k, here, n, of):
            return lax.rem(here - of(k) + n, n)

        def kx_of(k):
            return lax.div(k, nz)

        def kz_of(k):
            return lax.rem(k, nz)

        iz_down.wait()
        ix_down.wait()
        from_x = {}
        from_z = {}
        for p in range(2):
            for r in range(2):
                for d in range(nz):
                    from_x[d, p, r] = place(SZ[(nz - d) % nz, 0, 2 * r + p], x, nx, kx_of)
                for d in range(nx):
                    from_z[d, p, r] = place(SX[(nx - d) % nx, 0, 2 * r + p], z, nz, kz_of)

        def hand_on(name, held, packed, landed, where, n, at):
            order = far_first(n) + [0]
            for d in order:
                for p in range(2):
                    for r in range(2):
                        packed[2 * d + p, r] = held[where[d, p, r]]
            for d in order[:-1]:
                for p in range(2):
                    send(name, packed.at[2 * d + p], landed.at[2 * d + core], at(d, p))
            send(name, packed.at[other], landed.at[core], at(0, other))
            landed[core] = packed[core]

        taken("ca1", recv_sem, GCA.at[pl.ds(0, nx - 1)])
        hand_on("ca2", GCA, PCA, RCA, from_x, nz, at_z)
        taken("cb1", recv_sem, GCB.at[pl.ds(0, nz - 1)])
        hand_on("cb2", GCB, PCB, RCB, from_z, nx, at_x)
        taken("e1", recv_sem, GE.at[pl.ds(0, nx - 1)])
        hand_on("e2", GE, PE, RE, from_x, nz, at_z)
        taken("va1", recv_sem, GVA.at[pl.ds(0, nx - 1)])
        hand_on("va2", GVA, PVA, RVA, from_x, nz, at_z)
        taken("vb1", recv_sem, GVB.at[pl.ds(0, nz - 1)])
        hand_on("vb2", GVB, PVB, RVB, from_z, nx, at_x)

        mine = []
        for ref in (first_ref, second_ref):
            k = ref[0, core]
            mine.append((place(k, z, nz, kz_of), place(k, x, nx, kx_of)))

        taken("ca2", recv_sem, RCA.at[pl.ds(0, 2 * nz - 1)])
        for r in range(2):
            for c in range(2):
                CB[0, c, r, 0:16, :] = RCA[2 * mine[r][0] + c, r]
        taken("cb2", recv_sem, RCB.at[pl.ds(0, 2 * nx - 1)])
        for r in range(2):
            for c in range(2):
                CB[0, c, r, 16:32, :] = RCB[2 * mine[r][1] + c, r]
        for d in far_first(ny):
            send(f"y{d}", CB.at[0], CB.at[d], at_y(d, core))
        taken("e2", recv_sem, RE.at[pl.ds(0, 2 * nz - 1)])
        for r in range(2):
            for c in range(2):
                EB[0, c, r] = RE[2 * mine[r][0] + c, r]
        for d in far_first(ny):
            send("ye", EB.at[0], EB.at[d], at_y(d, core))
        loads[3].wait()
        taken("w", recv_sem, W.at[0])

        def y_from(k):
            return lax.rem(y - k + ny, ny)

        def block(k):
            row = pl.multiple_of(y_from(k) * (2 * PT), 2 * PT)
            w = jnp.concatenate([W[0, pl.ds(row, 2 * PT), :], W[1, pl.ds(row, 2 * PT), :]], axis=1)
            c1 = jnp.concatenate([CB[k, 0, 0], CB[k, 1, 0]], axis=1).astype(F32)
            c2 = jnp.concatenate([CB[k, 0, 1], CB[k, 1, 1]], axis=1).astype(F32)
            for b in range(4):
                rho = jnp.concatenate(
                    [(c1[c : c + 1, :] * c2).astype(BF16) for c in range(8 * b, 8 * b + 8)], axis=0
                )
                part = jnp.dot(rho, w, preferred_element_type=F32)
                for lane in range(2):
                    piece = part[:, 128 * lane : 128 * lane + 128]
                    if k == 0:
                        S[lane, pl.ds(256 * b, 256), :] = piece
                    else:
                        S[lane, pl.ds(256 * b, 256), :] += piece

        block(0)
        near_first = sorted(range(1, ny), key=lambda d: (min(d, ny - d), d))
        for d in near_first:
            taken(f"y{d}", recv_sem, CB.at[0])
            block(d)
        taken("va2", recv_sem, RVA.at[pl.ds(0, 2 * nz - 1)])
        taken("vb2", recv_sem, RVB.at[pl.ds(0, 2 * nx - 1)])
        vals = []
        for r in range(2):
            halves = []
            for c in range(2):
                top = RVA[2 * mine[r][0] + c, r]
                low = RVB[2 * mine[r][1] + c, r]
                both = jnp.concatenate([top, low], axis=0)
                V32[r, c] = both.astype(F32)
                halves.append(both)
            vals.append(jnp.concatenate(halves, axis=1))
        taken("ye", recv_sem, EB.at[pl.ds(0, ny - 1)])
        for k in range(ny):
            for c in range(2):
                row = pl.multiple_of((y_from(k) * 2 + c) * 8, 8)
                for role in (0, 1):
                    E32[role, pl.ds(row, 8), :] = EB[k, c, role].astype(F32)
        nw = 4 * ny
        for role, out in ((0, Y1), (1, Y2)):
            for q in range(4):
                eq = E32[role, pl.ds(q, nw, stride=4), :].astype(BF16)
                out[pl.ds(q * 128, 128), :] = lax.dot_general(
                    eq, vals[role][0:nw], (((0,), (0,)), ((), ())), preferred_element_type=F32
                )
        Zb[...] = jnp.zeros_like(Zb)

        def z_block(i, carry):
            for lane in range(2):
                cols = pl.ds(lane * 128, 128)
                y1 = [Y1[pl.ds(pl.multiple_of((i * 8 + c) * NE, NE), NE), cols] for c in range(8)]

                def over_d(d, acc):
                    at = pl.multiple_of(d * NE, NE)
                    y2 = Y2[pl.ds(at, NE), cols]
                    mirror = pl.multiple_of((d + 7 - 2 * lax.rem(d, 8)) * NE, NE)
                    zb = Zb[pl.ds(mirror, NE), cols]
                    new = []
                    for c in range(8):
                        s = S[lane, pl.ds((i * 8 + c) * NB + d, 1), :]
                        new.append(acc[c] + s * y2)
                        zb = zb + s * y1[c]
                    Zb[pl.ds(mirror, NE), cols] = zb
                    return tuple(new)

                zero = tuple(jnp.zeros((NE, 128), F32) for c in range(8))
                acc = lax.fori_loop(0, NB, over_d, zero)
                for c in range(8):
                    Zf[pl.ds(pl.multiple_of((i * 8 + 7 - c) * NE, NE), NE), cols] = acc[c]
            return carry

        lax.fori_loop(0, 4, z_block, 0)

        for fb, Z, role in ((0, Zf, 0), (1, Zb, 1)):
            v = jnp.concatenate(
                [
                    jnp.concatenate(
                        [V32[role, lane, pl.ds(i, 16, stride=2), :] for lane in range(2)], axis=1
                    )
                    for i in range(2)
                ],
                axis=0,
            ).astype(BF16)
            for h in range(4):
                f = lax.dot_general(
                    v, Z[pl.ds(h * 128, 128), :].astype(BF16), (((1,), (1,)), ((), ())),
                    preferred_element_type=F32,
                )
                for i in range(2):
                    T32[pl.ds(fb * 8 + h * 2 + i, 16, stride=16), :] = f[16 * i : 16 * i + 16, :]
        for s in range(n_scr):
            SB[s] = T32[pl.ds(16 * s, 16), :].astype(BF16)
        for d in far_first(ny) + [0]:
            for c in (core, other):
                to = lax.rem(y + d, ny) * 2 + c
                if d > 0 or c is other:
                    send("sum", SB.at[to], RB.at[core * ny + d], (g, to))
        RB[core * ny] = SB[sc]
        for name, like in (
            ("ix", IX.at[pl.ds(0, nx - 1)]), ("iz", IZ.at[pl.ds(0, nz - 1)]),
            ("ca1", GCA.at[pl.ds(0, nx - 1)]), ("cb1", GCB.at[pl.ds(0, nz - 1)]),
            ("e1", GE.at[pl.ds(0, nx - 1)]),
            ("va1", GVA.at[pl.ds(0, nx - 1)]), ("vb1", GVB.at[pl.ds(0, nz - 1)]),
            ("w", W.at[0]),
            ("ca2", RCA.at[pl.ds(0, 2 * nz - 1)]), ("cb2", RCB.at[pl.ds(0, 2 * nx - 1)]),
            ("e2", RE.at[pl.ds(0, 2 * nz - 1)]),
            ("va2", RVA.at[pl.ds(0, 2 * nz - 1)]), ("vb2", RVB.at[pl.ds(0, 2 * nx - 1)]),
            ("ye", EB.at[pl.ds(0, ny - 1)]), ("sum", RB.at[pl.ds(0, n_scr - 1)]),
        ):
            taken(name, send_sem, like)
        for d in range(1, ny):
            taken(f"y{d}", send_sem, CB.at[0])
        taken("sum", recv_sem, RB.at[pl.ds(0, n_scr - 1)])
        O32[...] = jnp.zeros_like(O32)
        for p in range(2):
            live = jnp.where(p < cnt_ref[0], 1.0, 0.0).astype(F32)
            tot = RB[p * ny].astype(F32)
            for d in range(1, ny):
                tot = tot + RB[p * ny + d].astype(F32)
            tot = tot * live
            for fb, out in ((0, fwd_ref), (1, back_ref)):
                for i in range(2):
                    for h in range(4):
                        r = fb * 8 + h * 2 + i
                        row = jnp.broadcast_to(tot[r : r + 1, :], (8, 128))
                        O32[pl.ds(i * 32 + h * 8, 8), :] = pltpu.roll(
                            pltpu.roll(row, NE, 1), 0, 1, stride=NE, stride_axis=0
                        )
                out[p] = O32[...].T[0:NE, 0:64]

    def run(wave_val, wave_con, excite, screening, pair_count, pair_kpoint, pair_partner):
        vmem = pl.BlockSpec(memory_space=pltpu.VMEM)
        smem = pl.BlockSpec(memory_space=pltpu.SMEM)
        hbm = pl.BlockSpec(memory_space=pl.ANY)
        n_mu = 2 * PT * ny
        shape = jax.ShapeDtypeStruct((2, NE, 64), F32)
        V = pltpu.VMEM
        fwd, back = pl.pallas_call(
            kernel,
            out_shape=(shape, shape),
            in_specs=[hbm, hbm, hbm, hbm, smem, smem, smem],
            out_specs=(vmem, vmem),
            scratch_shapes=[
                V((2, n_mu, PT), BF16),
                V((NB, PT), BF16), V((NB, PT), BF16), V((NE, 64), BF16),
                V((1, 128), jnp.int32), V((nx, 1, 128), jnp.int32), V((nz, 1, 128), jnp.int32),
                pltpu.SMEM((nx, 1, 128), jnp.int32), pltpu.SMEM((nz, 1, 128), jnp.int32),
                V((nx, 16, PT), BF16), V((nz, 16, PT), BF16),
                V((nx, 16, PT), BF16), V((nz, 16, PT), BF16), V((nx, 8, PT), BF16),
                V((2 * nz, 2, 16, PT), BF16), V((2 * nx, 2, 16, PT), BF16),
                V((2 * nz, 2, 16, PT), BF16), V((2 * nx, 2, 16, PT), BF16), V((2 * nz, 2, 8, PT), BF16),
                V((2 * nz, 2, 16, PT), BF16), V((2 * nx, 2, 16, PT), BF16),
                V((2 * nz, 2, 16, PT), BF16), V((2 * nx, 2, 16, PT), BF16), V((2 * nz, 2, 8, PT), BF16),
                V((ny, 2, 2, NB, PT), BF16), V((ny, 2, 2, 8, PT), BF16),
                V((16, 128), F32), V((128, 128), F32),
                V((2, NB * NB, PT), F32),
                V((2, 16 * ny, 128), F32),
                V((DE, 2 * PT), F32), V((DE, 2 * PT), F32),
                V((2, 2, NB, PT), F32),
                V((DE, 2 * PT), F32), V((DE, 2 * PT), F32),
                V((256, 128), F32), V((16, 16, 128), BF16), V((n_scr, 16, 128), BF16),
                V((128, 128), F32),
                pltpu.SemaphoreType.DMA((n_groups,)), pltpu.SemaphoreType.DMA((n_groups,)),
                pltpu.SemaphoreType.DMA((4,)),
            ],
            compiler_params=pltpu.CompilerParams(
                collective_id=0, has_side_effects=True, vmem_limit_bytes=60 * 1024 * 1024
            ),
        )(
            wave_val[0], wave_con[0], jnp.transpose(excite[0]), screening[0],
            pair_count, pair_kpoint, pair_partner,
        )
        return jnp.swapaxes(fwd, 1, 2)[None], jnp.swapaxes(back, 1, 2)[None]

    return run


def solution(mesh, sides=None):
    side = math.isqrt(mesh.shape["kgrp"])
    nx, nz = sides or (side, side)
    return jax.shard_map(
        build(nx, nz, mesh.shape["scr"] // 2),
        mesh=mesh,
        in_specs=(
            P("kgrp", None, "scr"),
            P("kgrp", None, "scr"),
            P("kgrp", "scr", None),
            P("kgrp", None, "scr"),
            P("kgrp"),
            P("kgrp", None),
            P("kgrp", None),
        ),
        out_specs=(P("kgrp", None, "scr", None), P("kgrp", None, "scr", None)),
        check_vma=False,
    )
```

time: 85.7 us -> 62 us (0.72)
  Pallas kernels: 79.8 us -> 58.5 us
  local copies, waits for them, and re-layouts: 4.29 us -> 1.94 us
    pallas_call x1, Pallas kernels: 79.8 us -> 58.5 us  [run(): pl.pallas_call(kernel, out_shape=(shape, shape), in_specs=[hbm, hbm, hbm,...]
    unnamed x14 -> x4, local copies, waits for them, and re-layouts: 4.29 us -> 1.94 us
where the time goes in v2:
time: 62 us; the launch traced here: 61.7 us
  Pallas kernels  58.5 us (94%)
  local copies, waits for them, and re-layouts  1.94 us (3%)
  between operations  1.29 us (2%)
    pallas_call x1, Pallas kernels, run(): pl.pallas_call(kernel, out_shape=(shape, shape), in_specs=[hbm, hbm, hbm,...  58.5 us
    unnamed x4, local copies, waits for them, and re-layouts  1.94 us

profile of v2, /device:TPU:1, one launch (start us, length us, event | category | flops | bytes accessed | tf_op | source)
XLA Modules:
  0.0 61.7 jit_solution(2258691193383239495)
XLA Ops:
  1.3 58.5 %shard_map.86 = (f32[2,16,64]{2,1,0:T(8,128)}, f32[2,16,64]{2,1,0:T(8,128)}) custom-call(bf16[32,128]{1,0:T(8,128)(2,1)} %bitcast.15, bf16[32,128]{1,0:T(8,128)(2,1)} %bitcast.16, bf16[16,64]{1,0:T(8,128)(2,1)} %bitcast.17, bf16[2048,128]{1,0:T(8,128)(2,1)} %bitcast.12, s32[1]{0:T(128)S(6)} %copy.11.cnt_ref, s32[1,2]{1,0:T(1,128)} %first_ref.1, ...), custom_call_target="tpu_custom_call" | custom-call | tf_op jit(solution)/shard_map/pallas_call | solution.py:336
  59.8 0.0 copy-start
  59.8 1.3 %copy.12 = f32[1,2,64,16]{2,3,1,0:T(8,128)} copy(f32[1,2,64,16]{2,3,1,0:T(8,128)} %bitcast.14) | data formatting | bytes 16384
  61.1 0.0 copy-done
  61.1 0.6 copy.13
Async XLA Ops:
  59.8 1.3 %copy-start = (f32[2,16,64]{2,1,0:T(8,128)S(1)}, f32[2,16,64]{2,1,0:T(8,128)}, u32[]{:S(2)}) copy-start(f32[2,16,64]{2,1,0:T(8,128)} %get-tuple-element.5) | copy-start | bytes 24580

commit v3 on v2

--- a/solution.py
+++ b/solution.py
@@ -19,13 +19,13 @@
 
 def build(nx, nz, ny):
     n_scr = 2 * ny
-    n_groups = 14 + ny
+    n_groups = 8 + 10 + 3 * ny + 1
 
     def kernel(
         val_ref, con_ref, exc_ref, scr_ref, cnt_ref, first_ref, second_ref,
         fwd_ref, back_ref,
         W, con_v, val_v, exc_v, own_i, IX, IZ, SX, SZ,
-        GCA, GCB, GVA, GVB, GE, PCA, PCB, PVA, PVB, PE, RCA, RCB, RVA, RVB, RE,
+        GCA, GCB, GVA, GVB, GE, PCA, PCB, PVA, PVB, PE, RCA0, RCA1, RCB0, RCB1, RVA0, RVA1, RVB0, RVB1, RE0, RE1,
         CB, EB, xt, xr, S, E32, Y1, Y2, V32, Zf, Zb, T32, SB, RB, O32,
         send_sem, recv_sem, local_sem,
     ):
@@ -48,6 +48,8 @@
 
         def far_first(n):
             return sorted(range(1, n), key=lambda d: -min(d, n - d))
+
+        RCA, RCB, RVA, RVB, RE = (RCA0, RCA1), (RCB0, RCB1), (RVA0, RVA1), (RVB0, RVB1), (RE0, RE1)
 
         loads = [
             pltpu.make_async_copy(src, dst, local_sem.at[i])
@@ -74,7 +76,11 @@
             ).start()
 
         def taken(name, sems, like):
-            pltpu.make_async_copy(like, like, sems.at[groups[name]]).wait()
+            if name in groups:
+                pltpu.make_async_copy(like, like, sems.at[groups[name]]).wait()
+
+        def first(buf, n):
+            return buf.at[pl.ds(0, max(n, 1))]
 
         lane = lax.broadcasted_iota(jnp.int32, (1, 128), 1)
         row = jnp.zeros((1, 128), jnp.int32)
@@ -117,10 +123,10 @@
             send("vb1", val_v.at[pl.ds(16, 16)], GVB.at[d], at_z(d, core))
         send("w", scr_ref, W.at[core], at_y(0, other))
 
-        taken("ix", recv_sem, IX.at[pl.ds(0, nx - 1)])
+        taken("ix", recv_sem, first(IX, nx - 1))
         ix_down = pltpu.make_async_copy(IX, SX, local_sem.at[0])
         ix_down.start()
-        taken("iz", recv_sem, IZ.at[pl.ds(0, nz - 1)])
+        taken("iz", recv_sem, first(IZ, nz - 1))
         iz_down = pltpu.make_async_copy(IZ, SZ, local_sem.at[1])
         iz_down.start()
 
@@ -144,50 +150,85 @@
                 for d in range(nx):
                     from_z[d, p, r] = place(SX[(nx - d) % nx, 0, 2 * r + p], z, nz, kz_of)
 
-        def hand_on(name, held, packed, landed, where, n, at):
+        def hand_on(name, roles, held, packed, landed, where, n, at):
             order = far_first(n) + [0]
             for d in order:
                 for p in range(2):
-                    for r in range(2):
-                        packed[2 * d + p, r] = held[where[d, p, r]]
-            for d in order[:-1]:
-                for p in range(2):
-                    send(name, packed.at[2 * d + p], landed.at[2 * d + core], at(d, p))
-            send(name, packed.at[other], landed.at[core], at(0, other))
-            landed[core] = packed[core]
-
-        taken("ca1", recv_sem, GCA.at[pl.ds(0, nx - 1)])
-        hand_on("ca2", GCA, PCA, RCA, from_x, nz, at_z)
-        taken("cb1", recv_sem, GCB.at[pl.ds(0, nz - 1)])
-        hand_on("cb2", GCB, PCB, RCB, from_z, nx, at_x)
-        taken("e1", recv_sem, GE.at[pl.ds(0, nx - 1)])
-        hand_on("e2", GE, PE, RE, from_x, nz, at_z)
-        taken("va1", recv_sem, GVA.at[pl.ds(0, nx - 1)])
-        hand_on("va2", GVA, PVA, RVA, from_x, nz, at_z)
-        taken("vb1", recv_sem, GVB.at[pl.ds(0, nz - 1)])
-        hand_on("vb2", GVB, PVB, RVB, from_z, nx, at_x)
+                    for r in roles:
+                        packed[r, 2 * d + p] = held[where[d, p, r]]
+            for r in roles:
+                for d in order[:-1]:
+                    for p in range(2):
+                        send(f"{name}{r}", packed.at[r, 2 * d + p], landed[r].at[2 * d + core], at(d, p))
+                send(f"{name}{r}", packed.at[r, other], landed[r].at[core], at(0, other))
+                landed[r][core] = packed[r, core]
+
+        taken("ca1", recv_sem, first(GCA, nx - 1))
+        hand_on("ca2", (0,), GCA, PCA, RCA, from_x, nz, at_z)
+        taken("cb1", recv_sem, first(GCB, nz - 1))
+        hand_on("cb2", (0,), GCB, PCB, RCB, from_z, nx, at_x)
+        hand_on("ca2", (1,), GCA, PCA, RCA, from_x, nz, at_z)
+        hand_on("cb2", (1,), GCB, PCB, RCB, from_z, nx, at_x)
+        taken("e1", recv_sem, first(GE, nx - 1))
+        hand_on("e2", (0, 1), GE, PE, RE, from_x, nz, at_z)
 
         mine = []
         for ref in (first_ref, second_ref):
             k = ref[0, core]
             mine.append((place(k, z, nz, kz_of), place(k, x, nx, kx_of)))
 
-        taken("ca2", recv_sem, RCA.at[pl.ds(0, 2 * nz - 1)])
+        class Spread:
+            def __init__(self, name, buf):
+                self.name, self.buf = name, buf
+
+            def begin(self):
+                for d in [d for d in far_first(ny) if min(d, ny - d) <= 2]:
+                    send(f"{self.name}{d}", self.buf(0), self.buf(d), at_y(d, core))
+
+            def relay(self):
+                if ny < 8:
+                    return
+                for d, step, half in ((2, 1, 0), (6, 7, 1)):
+                    self.take(d)
+                    at2, at1 = (2 * step) % ny, step
+                    send(f"{self.name}4{half}", self.buf(d, half), self.buf(4, half), at_y(at2, core))
+                    far = (d + step) % ny
+                    send(f"{self.name}{far}", self.buf(d), self.buf(far), at_y(at1, core))
+
+            def take(self, d, sems=recv_sem):
+                if d == 4 and ny == 8:
+                    for half in range(2):
+                        taken(f"{self.name}4{half}", sems, self.buf(4, half))
+                else:
+                    taken(f"{self.name}{d}", sems, self.buf(d))
+
+        def view_of(buf, r):
+            def view(d, half=None):
+                return buf.at[r, d] if half is None else buf.at[r, d, half]
+            return view
+
+        rings = [Spread("y0", view_of(CB, 0)), Spread("y1", view_of(CB, 1)), Spread("ye", view_of(EB, 0))]
+
         for r in range(2):
+            taken(f"ca2{r}", recv_sem, first(RCA[r], 2 * nz - 1))
             for c in range(2):
-                CB[0, c, r, 0:16, :] = RCA[2 * mine[r][0] + c, r]
-        taken("cb2", recv_sem, RCB.at[pl.ds(0, 2 * nx - 1)])
+                CB[r, 0, c, 0:16, :] = RCA[r][2 * mine[r][0] + c]
+            taken(f"cb2{r}", recv_sem, first(RCB[r], 2 * nx - 1))
+            for c in range(2):
+                CB[r, 0, c, 16:32, :] = RCB[r][2 * mine[r][1] + c]
+            rings[r].begin()
+        taken("va1", recv_sem, first(GVA, nx - 1))
+        hand_on("va2", (0, 1), GVA, PVA, RVA, from_x, nz, at_z)
+        taken("vb1", recv_sem, first(GVB, nz - 1))
+        hand_on("vb2", (0, 1), GVB, PVB, RVB, from_z, nx, at_x)
         for r in range(2):
+            taken(f"e2{r}", recv_sem, first(RE[r], 2 * nz - 1))
             for c in range(2):
-                CB[0, c, r, 16:32, :] = RCB[2 * mine[r][1] + c, r]
-        for d in far_first(ny):
-            send(f"y{d}", CB.at[0], CB.at[d], at_y(d, core))
-        taken("e2", recv_sem, RE.at[pl.ds(0, 2 * nz - 1)])
-        for r in range(2):
-            for c in range(2):
-                EB[0, c, r] = RE[2 * mine[r][0] + c, r]
-        for d in far_first(ny):
-            send("ye", EB.at[0], EB.at[d], at_y(d, core))
+                EB[0, 0, c, r] = RE[r][2 * mine[r][0] + c]
+        rings[2].begin()
+        rings[0].relay()
+        rings[1].relay()
+        rings[2].relay()
         loads[3].wait()
         taken("w", recv_sem, W.at[0])
 
@@ -197,8 +238,8 @@
         def block(k):
             row = pl.multiple_of(y_from(k) * (2 * PT), 2 * PT)
             w = jnp.concatenate([W[0, pl.ds(row, 2 * PT), :], W[1, pl.ds(row, 2 * PT), :]], axis=1)
-            c1 = jnp.concatenate([CB[k, 0, 0], CB[k, 1, 0]], axis=1).astype(F32)
-            c2 = jnp.concatenate([CB[k, 0, 1], CB[k, 1, 1]], axis=1).astype(F32)
+            c1 = jnp.concatenate([CB[0, k, 0], CB[0, k, 1]], axis=1).astype(F32)
+            c2 = jnp.concatenate([CB[1, k, 0], CB[1, k, 1]], axis=1).astype(F32)
             for b in range(4):
                 rho = jnp.concatenate(
                     [(c1[c : c + 1, :] * c2).astype(BF16) for c in range(8 * b, 8 * b + 8)], axis=0
@@ -214,26 +255,31 @@
         block(0)
         near_first = sorted(range(1, ny), key=lambda d: (min(d, ny - d), d))
         for d in near_first:
-            taken(f"y{d}", recv_sem, CB.at[0])
+            for r in range(2):
+                if ny < 8 or d not in (2, 6):
+                    rings[r].take(d)
             block(d)
-        taken("va2", recv_sem, RVA.at[pl.ds(0, 2 * nz - 1)])
-        taken("vb2", recv_sem, RVB.at[pl.ds(0, 2 * nx - 1)])
+        for r in range(2):
+            taken(f"va2{r}", recv_sem, first(RVA[r], 2 * nz - 1))
+            taken(f"vb2{r}", recv_sem, first(RVB[r], 2 * nx - 1))
         vals = []
         for r in range(2):
             halves = []
             for c in range(2):
-                top = RVA[2 * mine[r][0] + c, r]
-                low = RVB[2 * mine[r][1] + c, r]
+                top = RVA[r][2 * mine[r][0] + c]
+                low = RVB[r][2 * mine[r][1] + c]
                 both = jnp.concatenate([top, low], axis=0)
                 V32[r, c] = both.astype(F32)
                 halves.append(both)
             vals.append(jnp.concatenate(halves, axis=1))
-        taken("ye", recv_sem, EB.at[pl.ds(0, ny - 1)])
+        for d in near_first:
+            if ny < 8 or d not in (2, 6):
+                rings[2].take(d)
         for k in range(ny):
             for c in range(2):
                 row = pl.multiple_of((y_from(k) * 2 + c) * 8, 8)
                 for role in (0, 1):
-                    E32[role, pl.ds(row, 8), :] = EB[k, c, role].astype(F32)
+                    E32[role, pl.ds(row, 8), :] = EB[0, k, c, role].astype(F32)
         nw = 4 * ny
         for role, out in ((0, Y1), (1, Y2)):
             for q in range(4):
@@ -252,17 +298,19 @@
                     at = pl.multiple_of(d * NE, NE)
                     y2 = Y2[pl.ds(at, NE), cols]
                     mirror = pl.multiple_of((d + 7 - 2 * lax.rem(d, 8)) * NE, NE)
-                    zb = Zb[pl.ds(mirror, NE), cols]
                     new = []
+                    terms = [Zb[pl.ds(mirror, NE), cols]]
                     for c in range(8):
                         s = S[lane, pl.ds((i * 8 + c) * NB + d, 1), :]
                         new.append(acc[c] + s * y2)
-                        zb = zb + s * y1[c]
-                    Zb[pl.ds(mirror, NE), cols] = zb
+                        terms.append(s * y1[c])
+                    while len(terms) > 1:
+                        terms = [sum(terms[j : j + 2][1:], terms[j]) for j in range(0, len(terms), 2)]
+                    Zb[pl.ds(mirror, NE), cols] = terms[0]
                     return tuple(new)
 
                 zero = tuple(jnp.zeros((NE, 128), F32) for c in range(8))
-                acc = lax.fori_loop(0, NB, over_d, zero)
+                acc = lax.fori_loop(0, NB, over_d, zero, unroll=4)
                 for c in range(8):
                     Zf[pl.ds(pl.multiple_of((i * 8 + 7 - c) * NE, NE), NE), cols] = acc[c]
             return carry
@@ -295,20 +343,24 @@
                     send("sum", SB.at[to], RB.at[core * ny + d], (g, to))
         RB[core * ny] = SB[sc]
         for name, like in (
-            ("ix", IX.at[pl.ds(0, nx - 1)]), ("iz", IZ.at[pl.ds(0, nz - 1)]),
-            ("ca1", GCA.at[pl.ds(0, nx - 1)]), ("cb1", GCB.at[pl.ds(0, nz - 1)]),
-            ("e1", GE.at[pl.ds(0, nx - 1)]),
-            ("va1", GVA.at[pl.ds(0, nx - 1)]), ("vb1", GVB.at[pl.ds(0, nz - 1)]),
+            ("ix", first(IX, nx - 1)), ("iz", first(IZ, nz - 1)),
+            ("ca1", first(GCA, nx - 1)), ("cb1", first(GCB, nz - 1)),
+            ("e1", first(GE, nx - 1)),
+            ("va1", first(GVA, nx - 1)), ("vb1", first(GVB, nz - 1)),
             ("w", W.at[0]),
-            ("ca2", RCA.at[pl.ds(0, 2 * nz - 1)]), ("cb2", RCB.at[pl.ds(0, 2 * nx - 1)]),
-            ("e2", RE.at[pl.ds(0, 2 * nz - 1)]),
-            ("va2", RVA.at[pl.ds(0, 2 * nz - 1)]), ("vb2", RVB.at[pl.ds(0, 2 * nx - 1)]),
-            ("ye", EB.at[pl.ds(0, ny - 1)]), ("sum", RB.at[pl.ds(0, n_scr - 1)]),
+            ("sum", first(RB, n_scr - 1)),
         ):
             taken(name, send_sem, like)
-        for d in range(1, ny):
-            taken(f"y{d}", send_sem, CB.at[0])
-        taken("sum", recv_sem, RB.at[pl.ds(0, n_scr - 1)])
+        for r in range(2):
+            taken(f"ca2{r}", send_sem, first(RCA[r], 2 * nz - 1))
+            taken(f"cb2{r}", send_sem, first(RCB[r], 2 * nx - 1))
+            taken(f"e2{r}", send_sem, first(RE[r], 2 * nz - 1))
+            taken(f"va2{r}", send_sem, first(RVA[r], 2 * nz - 1))
+            taken(f"vb2{r}", send_sem, first(RVB[r], 2 * nx - 1))
+        for spread in rings:
+            for d in range(1, ny):
+                spread.take(d, send_sem)
+        taken("sum", recv_sem, first(RB, n_scr - 1))
         O32[...] = jnp.zeros_like(O32)
         for p in range(2):
             live = jnp.where(p < cnt_ref[0], 1.0, 0.0).astype(F32)
@@ -345,11 +397,14 @@
                 pltpu.SMEM((nx, 1, 128), jnp.int32), pltpu.SMEM((nz, 1, 128), jnp.int32),
                 V((nx, 16, PT), BF16), V((nz, 16, PT), BF16),
                 V((nx, 16, PT), BF16), V((nz, 16, PT), BF16), V((nx, 8, PT), BF16),
-                V((2 * nz, 2, 16, PT), BF16), V((2 * nx, 2, 16, PT), BF16),
-                V((2 * nz, 2, 16, PT), BF16), V((2 * nx, 2, 16, PT), BF16), V((2 * nz, 2, 8, PT), BF16),
-                V((2 * nz, 2, 16, PT), BF16), V((2 * nx, 2, 16, PT), BF16),
-                V((2 * nz, 2, 16, PT), BF16), V((2 * nx, 2, 16, PT), BF16), V((2 * nz, 2, 8, PT), BF16),
-                V((ny, 2, 2, NB, PT), BF16), V((ny, 2, 2, 8, PT), BF16),
+                V((2, 2 * nz, 16, PT), BF16), V((2, 2 * nx, 16, PT), BF16),
+                V((2, 2 * nz, 16, PT), BF16), V((2, 2 * nx, 16, PT), BF16), V((2, 2 * nz, 8, PT), BF16),
+                V((2 * nz, 16, PT), BF16), V((2 * nz, 16, PT), BF16),
+                V((2 * nx, 16, PT), BF16), V((2 * nx, 16, PT), BF16),
+                V((2 * nz, 16, PT), BF16), V((2 * nz, 16, PT), BF16),
+                V((2 * nx, 16, PT), BF16), V((2 * nx, 16, PT), BF16),
+                V((2 * nz, 8, PT), BF16), V((2 * nz, 8, PT), BF16),
+                V((2, ny, 2, NB, PT), BF16), V((1, ny, 2, 2, 8, PT), BF16),
                 V((16, 128), F32), V((128, 128), F32),
                 V((2, NB * NB, PT), F32),
                 V((2, 16 * ny, 128), F32),

time: 62 us -> 56.6 us (0.913)
  Pallas kernels: 58.5 us -> 53.1 us
    pallas_call x1, Pallas kernels: 58.5 us -> 53.1 us  [run(): pl.pallas_call(kernel, out_shape=(shape, shape), in_specs=[hbm, hbm, hbm,...]
where the time goes in v3:
time: 56.6 us; the launch traced here: 56.3 us
  Pallas kernels  53.1 us (94%)
  local copies, waits for them, and re-layouts  1.94 us (3%)
  between operations  1.29 us (2%)
    pallas_call x1, Pallas kernels, run(): pl.pallas_call(kernel, out_shape=(shape, shape), in_specs=[hbm, hbm, hbm,...  53.1 us
    unnamed x4, local copies, waits for them, and re-layouts  1.94 us

profile of v3, /device:TPU:1, one launch (start us, length us, event | category | flops | bytes accessed | tf_op | source)
XLA Modules:
  0.0 56.3 jit_solution(11484809084750479551)
XLA Ops:
  1.3 53.1 %shard_map.86 = (f32[2,16,64]{2,1,0:T(8,128)}, f32[2,16,64]{2,1,0:T(8,128)}) custom-call(bf16[32,128]{1,0:T(8,128)(2,1)} %bitcast.15, bf16[32,128]{1,0:T(8,128)(2,1)} %bitcast.16, bf16[16,64]{1,0:T(8,128)(2,1)} %bitcast.17, bf16[2048,128]{1,0:T(8,128)(2,1)} %bitcast.12, s32[1]{0:T(128)S(6)} %copy.11.cnt_ref, s32[1,2]{1,0:T(1,128)} %first_ref.1, ...), custom_call_target="tpu_custom_call" | custom-call | tf_op jit(solution)/shard_map/pallas_call | solution.py:388
  54.4 0.0 copy-start
  54.4 1.3 %copy.12 = f32[1,2,64,16]{2,3,1,0:T(8,128)} copy(f32[1,2,64,16]{2,3,1,0:T(8,128)} %bitcast.14) | data formatting | bytes 16384
  55.7 0.0 copy-done
  55.7 0.6 %copy.13 = f32[1,2,64,16]{2,3,1,0:T(8,128)} copy(f32[1,2,64,16]{2,3,1,0:T(8,128)S(1)} %bitcast.13) | data formatting | bytes 16384
Async XLA Ops:
  54.4 1.3 %copy-start = (f32[2,16,64]{2,1,0:T(8,128)S(1)}, f32[2,16,64]{2,1,0:T(8,128)}, u32[]{:S(2)}) copy-start(f32[2,16,64]{2,1,0:T(8,128)} %get-tuple-element.5) | copy-start | bytes 24580

commit v4 on v3

--- a/solution.py
+++ b/solution.py
@@ -19,11 +19,11 @@
 
 def build(nx, nz, ny):
     n_scr = 2 * ny
-    n_groups = 8 + 10 + 3 * ny + 1
+    n_groups = 34
 
     def kernel(
         val_ref, con_ref, exc_ref, scr_ref, cnt_ref, first_ref, second_ref,
-        fwd_ref, back_ref,
+        out_ref,
         W, con_v, val_v, exc_v, own_i, IX, IZ, SX, SZ,
         GCA, GCB, GVA, GVB, GE, PCA, PCB, PVA, PVB, PE, RCA0, RCA1, RCB0, RCB1, RVA0, RVA1, RVB0, RVB1, RE0, RE1,
         CB, EB, xt, xr, S, E32, Y1, Y2, V32, Zf, Zb, T32, SB, RB, O32,
@@ -67,17 +67,20 @@
             pl.semaphore_signal(barrier, inc=1, device_id=peer, device_id_type=MESH)
 
         groups = {}
+        sent = {0: 0, 1: 0}
 
         def send(name, src, dst, to):
             k = groups.setdefault(name, len(groups))
+            out = 0 if name == "w" else 1
+            sent[out] += math.prod(src.shape) * jnp.dtype(src.dtype).itemsize
             pltpu.make_async_remote_copy(
-                src_ref=src, dst_ref=dst, send_sem=send_sem.at[k], recv_sem=recv_sem.at[k],
+                src_ref=src, dst_ref=dst, send_sem=send_sem.at[out], recv_sem=recv_sem.at[k],
                 device_id=to, device_id_type=MESH,
             ).start()
 
-        def taken(name, sems, like):
+        def taken(name, like):
             if name in groups:
-                pltpu.make_async_copy(like, like, sems.at[groups[name]]).wait()
+                pltpu.make_async_copy(like, like, recv_sem.at[groups[name]]).wait()
 
         def first(buf, n):
             return buf.at[pl.ds(0, max(n, 1))]
@@ -123,10 +126,10 @@
             send("vb1", val_v.at[pl.ds(16, 16)], GVB.at[d], at_z(d, core))
         send("w", scr_ref, W.at[core], at_y(0, other))
 
-        taken("ix", recv_sem, first(IX, nx - 1))
+        taken("ix", first(IX, nx - 1))
         ix_down = pltpu.make_async_copy(IX, SX, local_sem.at[0])
         ix_down.start()
-        taken("iz", recv_sem, first(IZ, nz - 1))
+        taken("iz", first(IZ, nz - 1))
         iz_down = pltpu.make_async_copy(IZ, SZ, local_sem.at[1])
         iz_down.start()
 
@@ -163,13 +166,13 @@
                 send(f"{name}{r}", packed.at[r, other], landed[r].at[core], at(0, other))
                 landed[r][core] = packed[r, core]
 
-        taken("ca1", recv_sem, first(GCA, nx - 1))
+        taken("ca1", first(GCA, nx - 1))
         hand_on("ca2", (0,), GCA, PCA, RCA, from_x, nz, at_z)
-        taken("cb1", recv_sem, first(GCB, nz - 1))
+        taken("cb1", first(GCB, nz - 1))
         hand_on("cb2", (0,), GCB, PCB, RCB, from_z, nx, at_x)
         hand_on("ca2", (1,), GCA, PCA, RCA, from_x, nz, at_z)
         hand_on("cb2", (1,), GCB, PCB, RCB, from_z, nx, at_x)
-        taken("e1", recv_sem, first(GE, nx - 1))
+        taken("e1", first(GE, nx - 1))
         hand_on("e2", (0, 1), GE, PE, RE, from_x, nz, at_z)
 
         mine = []
@@ -178,51 +181,62 @@
             mine.append((place(k, z, nz, kz_of), place(k, x, nx, kx_of)))
 
         class Spread:
-            def __init__(self, name, buf):
+            def __init__(self, name, buf, parts):
                 self.name, self.buf = name, buf
+                self.group = {d: part for part in parts for d in part}
+
+            def send(self, here, there, to, half=None):
+                name = f"{self.name}{self.group[there][0]}"
+                send(name, self.buf(here, half), self.buf(there, half), at_y(to, core))
 
             def begin(self):
                 for d in [d for d in far_first(ny) if min(d, ny - d) <= 2]:
-                    send(f"{self.name}{d}", self.buf(0), self.buf(d), at_y(d, core))
+                    self.send(0, d, d)
 
             def relay(self):
                 if ny < 8:
                     return
                 for d, step, half in ((2, 1, 0), (6, 7, 1)):
                     self.take(d)
-                    at2, at1 = (2 * step) % ny, step
-                    send(f"{self.name}4{half}", self.buf(d, half), self.buf(4, half), at_y(at2, core))
-                    far = (d + step) % ny
-                    send(f"{self.name}{far}", self.buf(d), self.buf(far), at_y(at1, core))
-
-            def take(self, d, sems=recv_sem):
-                if d == 4 and ny == 8:
-                    for half in range(2):
-                        taken(f"{self.name}4{half}", sems, self.buf(4, half))
-                else:
-                    taken(f"{self.name}{d}", sems, self.buf(d))
+                    self.send(d, 4, (2 * step) % ny, half)
+                    self.send(d, (d + step) % ny, step)
+
+            def take(self, d):
+                part = self.group[d]
+                if d == part[0]:
+                    taken(f"{self.name}{d}", self.buf(pl.ds(0, len(part))))
 
         def view_of(buf, r):
             def view(d, half=None):
                 return buf.at[r, d] if half is None else buf.at[r, d, half]
             return view
 
-        rings = [Spread("y0", view_of(CB, 0)), Spread("y1", view_of(CB, 1)), Spread("ye", view_of(EB, 0))]
+        near_first = sorted(range(1, ny), key=lambda d: (min(d, ny - d), d))
+        if ny == 8:
+            parts = ((2,), (6,), (1, 7), (3,), (5,), (4,))
+            parts_e = ((2,), (6,), (1, 7, 3, 5, 4))
+        else:
+            parts, parts_e = [(d,) for d in near_first], [tuple(near_first)]
+        rings = [
+            Spread("y0", view_of(CB, 0), parts),
+            Spread("y1", view_of(CB, 1), parts),
+            Spread("ye", view_of(EB, 0), parts_e),
+        ]
 
         for r in range(2):
-            taken(f"ca2{r}", recv_sem, first(RCA[r], 2 * nz - 1))
+            taken(f"ca2{r}", first(RCA[r], 2 * nz - 1))
             for c in range(2):
                 CB[r, 0, c, 0:16, :] = RCA[r][2 * mine[r][0] + c]
-            taken(f"cb2{r}", recv_sem, first(RCB[r], 2 * nx - 1))
+            taken(f"cb2{r}", first(RCB[r], 2 * nx - 1))
             for c in range(2):
                 CB[r, 0, c, 16:32, :] = RCB[r][2 * mine[r][1] + c]
             rings[r].begin()
-        taken("va1", recv_sem, first(GVA, nx - 1))
+        taken("va1", first(GVA, nx - 1))
         hand_on("va2", (0, 1), GVA, PVA, RVA, from_x, nz, at_z)
-        taken("vb1", recv_sem, first(GVB, nz - 1))
+        taken("vb1", first(GVB, nz - 1))
         hand_on("vb2", (0, 1), GVB, PVB, RVB, from_z, nx, at_x)
         for r in range(2):
-            taken(f"e2{r}", recv_sem, first(RE[r], 2 * nz - 1))
+            taken(f"e2{r}", first(RE[r], 2 * nz - 1))
             for c in range(2):
                 EB[0, 0, c, r] = RE[r][2 * mine[r][0] + c]
         rings[2].begin()
@@ -230,7 +244,7 @@
         rings[1].relay()
         rings[2].relay()
         loads[3].wait()
-        taken("w", recv_sem, W.at[0])
+        taken("w", W.at[0])
 
         def y_from(k):
             return lax.rem(y - k + ny, ny)
@@ -253,15 +267,14 @@
                         S[lane, pl.ds(256 * b, 256), :] += piece
 
         block(0)
-        near_first = sorted(range(1, ny), key=lambda d: (min(d, ny - d), d))
         for d in near_first:
             for r in range(2):
                 if ny < 8 or d not in (2, 6):
                     rings[r].take(d)
             block(d)
         for r in range(2):
-            taken(f"va2{r}", recv_sem, first(RVA[r], 2 * nz - 1))
-            taken(f"vb2{r}", recv_sem, first(RVB[r], 2 * nx - 1))
+            taken(f"va2{r}", first(RVA[r], 2 * nz - 1))
+            taken(f"vb2{r}", first(RVB[r], 2 * nx - 1))
         vals = []
         for r in range(2):
             halves = []
@@ -342,25 +355,11 @@
                 if d > 0 or c is other:
                     send("sum", SB.at[to], RB.at[core * ny + d], (g, to))
         RB[core * ny] = SB[sc]
-        for name, like in (
-            ("ix", first(IX, nx - 1)), ("iz", first(IZ, nz - 1)),
-            ("ca1", first(GCA, nx - 1)), ("cb1", first(GCB, nz - 1)),
-            ("e1", first(GE, nx - 1)),
-            ("va1", first(GVA, nx - 1)), ("vb1", first(GVB, nz - 1)),
-            ("w", W.at[0]),
-            ("sum", first(RB, n_scr - 1)),
-        ):
-            taken(name, send_sem, like)
-        for r in range(2):
-            taken(f"ca2{r}", send_sem, first(RCA[r], 2 * nz - 1))
-            taken(f"cb2{r}", send_sem, first(RCB[r], 2 * nx - 1))
-            taken(f"e2{r}", send_sem, first(RE[r], 2 * nz - 1))
-            taken(f"va2{r}", send_sem, first(RVA[r], 2 * nz - 1))
-            taken(f"vb2{r}", send_sem, first(RVB[r], 2 * nx - 1))
-        for spread in rings:
-            for d in range(1, ny):
-                spread.take(d, send_sem)
-        taken("sum", recv_sem, first(RB, n_scr - 1))
+        assert len(groups) <= n_groups
+        for out in range(2):
+            like = W.at[:, pl.ds(0, sent[out] // (4 * PT))]
+            pltpu.make_async_copy(like, like, send_sem.at[out]).wait()
+        taken("sum", first(RB, n_scr - 1))
         O32[...] = jnp.zeros_like(O32)
         for p in range(2):
             live = jnp.where(p < cnt_ref[0], 1.0, 0.0).astype(F32)
@@ -368,7 +367,7 @@
             for d in range(1, ny):
                 tot = tot + RB[p * ny + d].astype(F32)
             tot = tot * live
-            for fb, out in ((0, fwd_ref), (1, back_ref)):
+            for fb in range(2):
                 for i in range(2):
                     for h in range(4):
                         r = fb * 8 + h * 2 + i
@@ -376,20 +375,20 @@
                         O32[pl.ds(i * 32 + h * 8, 8), :] = pltpu.roll(
                             pltpu.roll(row, NE, 1), 0, 1, stride=NE, stride_axis=0
                         )
-                out[p] = O32[...].T[0:NE, 0:64]
+                out_ref[fb, p] = O32[...].T[0:NE, 0:64]
 
     def run(wave_val, wave_con, excite, screening, pair_count, pair_kpoint, pair_partner):
         vmem = pl.BlockSpec(memory_space=pltpu.VMEM)
         smem = pl.BlockSpec(memory_space=pltpu.SMEM)
         hbm = pl.BlockSpec(memory_space=pl.ANY)
         n_mu = 2 * PT * ny
-        shape = jax.ShapeDtypeStruct((2, NE, 64), F32)
+        shape = jax.ShapeDtypeStruct((2, 2, NE, 64), F32)
         V = pltpu.VMEM
-        fwd, back = pl.pallas_call(
+        both = pl.pallas_call(
             kernel,
-            out_shape=(shape, shape),
+            out_shape=shape,
             in_specs=[hbm, hbm, hbm, hbm, smem, smem, smem],
-            out_specs=(vmem, vmem),
+            out_specs=vmem,
             scratch_shapes=[
                 V((2, n_mu, PT), BF16),
                 V((NB, PT), BF16), V((NB, PT), BF16), V((NE, 64), BF16),
@@ -411,9 +410,9 @@
                 V((DE, 2 * PT), F32), V((DE, 2 * PT), F32),
                 V((2, 2, NB, PT), F32),
                 V((DE, 2 * PT), F32), V((DE, 2 * PT), F32),
-                V((256, 128), F32), V((16, 16, 128), BF16), V((n_scr, 16, 128), BF16),
+                V((256, 128), F32), V((n_scr, 16, 128), BF16), V((n_scr, 16, 128), BF16),
                 V((128, 128), F32),
-                pltpu.SemaphoreType.DMA((n_groups,)), pltpu.SemaphoreType.DMA((n_groups,)),
+                pltpu.SemaphoreType.DMA((2,)), pltpu.SemaphoreType.DMA((n_groups,)),
                 pltpu.SemaphoreType.DMA((4,)),
             ],
             compiler_params=pltpu.CompilerParams(
@@ -423,7 +422,8 @@
             wave_val[0], wave_con[0], jnp.transpose(excite[0]), screening[0],
             pair_count, pair_kpoint, pair_partner,
         )
-        return jnp.swapaxes(fwd, 1, 2)[None], jnp.swapaxes(back, 1, 2)[None]
+        both = jnp.swapaxes(both, 2, 3)
+        return both[0][None], both[1][None]
 
     return run
 

time: 56.6 us -> 55.6 us (0.982)
  local copies, waits for them, and re-layouts: 1.94 us -> 1.35 us
    unnamed x4 -> x0, local copies, waits for them, and re-layouts: 1.94 us -> none
    slice x0 -> x1, local copies, waits for them, and re-layouts: none -> 1.35 us  [run(): return (both[0][None], both[1][None])]
where the time goes in v4:
time: 55.6 us; the launch traced here: 55.3 us
  Pallas kernels  52.7 us (95%)
  local copies, waits for them, and re-layouts  1.35 us (2%)
  between operations  1.29 us (2%)
    pallas_call x1, Pallas kernels, run(): pl.pallas_call(kernel, out_shape=shape, in_specs=[hbm, hbm, hbm, hbm, sme...  52.7 us
    slice x1, local copies, waits for them, and re-layouts, run(): return (both[0][None], both[1][None])  1.35 us

profile of v4, /device:TPU:1, one launch (start us, length us, event | category | flops | bytes accessed | tf_op | source)
XLA Modules:
  0.0 55.3 jit_solution(17707621989097488662)
XLA Ops:
  1.3 52.7 %shard_map.86 = f32[2,2,16,64]{3,2,1,0:T(8,128)} custom-call(bf16[32,128]{1,0:T(8,128)(2,1)} %bitcast.9, bf16[32,128]{1,0:T(8,128)(2,1)} %bitcast.10, bf16[16,64]{1,0:T(8,128)(2,1)} %bitcast.11, bf16[2048,128]{1,0:T(8,128)(2,1)} %bitcast.7, s32[1]{0:T(128)S(6)} %copy.9.cnt_ref, s32[1,2]{1,0:T(1,128)} %first_ref.1, s32[1,2]{1,0:T(1,128)} %second_ref.1), custom_call_target="tpu_custom_call" | custom-call | tf_op jit(solution)/shard_map/pallas_call | solution.py:387
  54.0 1.3 %fusion = (f32[1,2,64,16]{2,3,1,0:T(8,128)}, f32[1,2,64,16]{2,3,1,0:T(8,128)}) fusion(f32[2,2,64,16]{2,3,1,0:T(8,128)} %bitcast.8), kind=kLoop, calls=%fused_computation | loop fusion | bytes 32768 | tf_op jit(solution)/shard_map/slice | solution.py:426
